TPU v7x, 32 devices: a whole 2x2x4 slice. The times are simulated.
32 devices in a mesh: groups: 1, rows: 32 (over z, y, x, core).
Axes of the slice: x: 2, y: 2, z: 4, core: 2. Of those that a mesh axis runs over, the one named last changes fastest.
Arguments:
- tokens: bfloat16 [384, 8192], P(('groups', 'rows')), may hold values from -6 to 6
- gate_weight: bfloat16 [8192, 14336], P('rows'), may hold values from -0.0625 to 0.0625
- up_weight: bfloat16 [8192, 14336], P('rows'), may hold values from -0.0625 to 0.0625
- skew_params: float32 [2, 2, 128, 64, 64], P(None, None, 'rows'), may hold values from -0.3125 to 0.3125
- section_bits: int32 [2, 13], replicated, may hold values from 0 to 12, each once within a row
- upstream: bfloat16 [384, 14336], P('groups', 'rows'), may hold values from -0.3125 to 0.3125
Outputs:
- activation: bfloat16 [384, 14336], P('groups', 'rows')
- skew_grad: float32 [2, 2, 128, 64, 64], P('groups', None, 'rows')
Inputs may be any that keep to these rules, and one draw needn't show every extreme that they name: Each row of section_bits names every one of the 13 bit positions once.
All inputs are finite; a program needn't handle non-finite values.
Results may differ from a plain program's by a relative error of at most 0.0093.
Values may be sent and summed in bfloat16 or wider, within the bound.
A program may use at most 192 MiB of HBM per device.

v0:
```python
import jax
import jax.numpy as jnp
from jax import lax
from jax.sharding import PartitionSpec as P


def cayley(skew_blocks):
    extent = skew_blocks.shape[-1]
    identity = jnp.eye(extent, dtype=jnp.float32)
    generator = skew_blocks - jnp.swapaxes(skew_blocks, -1, -2)
    minus_part = identity - generator
    squared = jnp.einsum(
        "...ij,...jk->...ik", minus_part, minus_part, precision=lax.Precision.HIGHEST
    )
    normal = identity - jnp.einsum(
        "...ij,...jk->...ik", generator, generator, precision=lax.Precision.HIGHEST
    )
    lower_factor = jnp.linalg.cholesky(normal)
    halfway = lax.linalg.triangular_solve(lower_factor, squared, left_side=True, lower=True)
    return lax.linalg.triangular_solve(
        lower_factor, halfway, left_side=True, lower=True, transpose_a=True
    )


def slot_order(section_row, extent):
    positions = jnp.arange(extent, dtype=jnp.int32)
    places = jnp.arange(section_row.shape[0], dtype=jnp.int32)
    digits = jnp.right_shift(positions[:, None], places[None, :]) & 1
    return jnp.sum(jnp.left_shift(digits, section_row[None, :]), axis=1)


def inverse_order(section_row, extent):
    positions = jnp.arange(extent, dtype=jnp.int32)
    places = jnp.arange(section_row.shape[0], dtype=jnp.int32)
    digits = jnp.right_shift(positions[:, None], section_row[None, :]) & 1
    return jnp.sum(jnp.left_shift(digits, places[None, :]), axis=1)


def rotate_columns(columns, rotation, orders, inverses):
    kept_inputs = []
    current = columns
    index = orders[0]
    block_count = rotation.shape[1]
    col_count = columns.shape[1]
    section_total = len(orders)
    for section_at in range(section_total):
        permuted = current[index]
        mixed_rows = jnp.einsum(
            "kji,kic->kjc",
            rotation[section_at],
            permuted.reshape(block_count, -1, col_count),
            preferred_element_type=jnp.float32,
        ).astype(jnp.bfloat16)
        kept_inputs.append(permuted)
        current = mixed_rows.reshape(columns.shape)
        if section_at + 1 < section_total:
            index = inverses[section_at][orders[section_at + 1]]
        else:
            index = inverses[section_at]
    return (current[index], kept_inputs)


def unrotate(grad_top, rotation, orders, inverses):
    block_count = rotation.shape[1]
    col_count = grad_top.shape[1]
    section_total = len(orders)
    slot_grads = [None] * section_total
    current = grad_top
    index = orders[section_total - 1]
    for section_at in reversed(range(section_total)):
        permuted = current[index]
        slot_grads[section_at] = permuted
        if section_at > 0:
            pulled = jnp.einsum(
                "kji,kjc->kic",
                rotation[section_at],
                permuted.reshape(block_count, -1, col_count),
                preferred_element_type=jnp.float32,
            ).astype(jnp.bfloat16)
            current = pulled.reshape(grad_top.shape)
            index = inverses[section_at][orders[section_at - 1]]
    return slot_grads


def block_products(slot_grad, slot_input, block_count):
    col_count = slot_grad.shape[-1]
    return jnp.einsum(
        "kjc,kic->kji",
        slot_grad.reshape(block_count, -1, col_count),
        slot_input.reshape(block_count, -1, col_count),
        preferred_element_type=jnp.float32,
    )


def shards(tokens, gate_weight, up_weight, skew_params, section_bits, upstream):
    extent = skew_params.shape[-1]
    model_width = tokens.shape[1]
    block_count = model_width // extent
    section_count = section_bits.shape[0]
    own_rotation, pullback = jax.vjp(cayley, skew_params)
    rotation = lax.all_gather(own_rotation.astype(jnp.bfloat16), "rows", axis=2, tiled=True)
    orders = [
        slot_order(section_bits[section_at], model_width) for section_at in range(section_count)
    ]
    inverses = [
        inverse_order(section_bits[section_at], model_width) for section_at in range(section_count)
    ]
    all_tokens = lax.all_gather(tokens, "rows", axis=0, tiled=True)
    gate_cols, up_cols = (
        lax.all_to_all(gate_weight, "rows", split_axis=1, concat_axis=0, tiled=True),
        lax.all_to_all(up_weight, "rows", split_axis=1, concat_axis=0, tiled=True),
    )
    rotated_gate, gate_inputs = rotate_columns(gate_cols, rotation[0], orders, inverses)
    rotated_up, up_inputs = rotate_columns(up_cols, rotation[1], orders, inverses)
    gate_pre = jnp.dot(all_tokens, rotated_gate, preferred_element_type=jnp.float32)
    up_pre = jnp.dot(all_tokens, rotated_up, preferred_element_type=jnp.float32)
    sigmoid_val = jax.nn.sigmoid(gate_pre)
    silu_val = gate_pre * sigmoid_val
    activation = (silu_val * up_pre).astype(jnp.bfloat16)
    cotangent = upstream.astype(jnp.float32)
    gate_grad = (cotangent * up_pre * sigmoid_val * (1.0 + gate_pre * (1.0 - sigmoid_val))).astype(
        jnp.bfloat16
    )
    up_grad = (cotangent * silu_val).astype(jnp.bfloat16)
    contract = (((0,), (0,)), ((), ()))
    gate_top = lax.dot_general(
        all_tokens, gate_grad, contract, preferred_element_type=jnp.float32
    ).astype(jnp.bfloat16)
    up_top = lax.dot_general(
        all_tokens, up_grad, contract, preferred_element_type=jnp.float32
    ).astype(jnp.bfloat16)
    gate_slots = unrotate(gate_top, rotation[0], orders, inverses)
    up_slots = unrotate(up_top, rotation[1], orders, inverses)
    gate_terms = jnp.stack(
        [
            block_products(gate_slots[section_at], gate_inputs[section_at], block_count)
            for section_at in range(section_count)
        ]
    )
    up_terms = jnp.stack(
        [
            block_products(up_slots[section_at], up_inputs[section_at], block_count)
            for section_at in range(section_count)
        ]
    )
    own_sums = lax.psum_scatter(
        jnp.stack((gate_terms, up_terms)), "rows", scatter_dimension=2, tiled=True
    )
    skew_grad = pullback(own_sums)[0]
    return (activation, skew_grad)


def solution(mesh):
    placed = (
        P(("groups", "rows"), None),
        P("rows", None),
        P("rows", None),
        P(None, None, "rows", None, None),
        P(),
        P("groups", "rows"),
    )
    return jax.shard_map(
        shards,
        mesh=mesh,
        in_specs=placed,
        out_specs=(P("groups", "rows"), P("groups", None, "rows", None, None)),
        check_vma=False,
    )
```

profile of v0, /device:TPU:0, one launch (start us, length us, event | category | flops | bytes accessed | tf_op | source)
XLA Modules:
  0.0 1387.2 jit_solution(2663491135916769819)
XLA Ops:
  7.2 10.2 copy.86
  17.4 7.4 all-to-all-start
  25.5 10.2 copy.88
  35.7 190.3 %all-to-all-done = bf16[256,32,448]{0,2,1:T(8,128)(2,1)} async-done(((bf16[256,32,448]{0,2,1:T(8,128)(2,1)}), bf16[256,32,448]{0,2,1:T(8,128)(2,1)}, u32[]{:S(2)}, u32[]{:S(2)}) %all-to-all-start) | async-done | bytes 7340064 | tf_op jit(solution)/shard_map/all_to_all | solution.py:110
  226.0 3.7 all-to-all-start.1
  231.0 93.8 %custom-call.14 = f32[2,2,4,64,64]{4,3,2,1,0:T(8,128)S(1)} custom-call(f32[2,2,4,64,64]{4,3,2,1,0:T(8,128)S(1)} %fusion.35), custom_call_target="Cholesky" | custom-call | tf_op jit(solution)/shard_map/jvp(jit(cholesky))/cholesky | solution.py:18
  326.7 78.6 %custom-call.22 = f32[2,2,4,1,64,64]{4,5,3,2,1,0:T(8,128)S(1)} custom-call(f32[2,2,4,1,64,64]{5,4,3,2,1,0:T(8,128)S(1)} %get-tuple-element.9), custom_call_target="InvertDiagBlocksLowerTriangular" | custom-call | tf_op jit(solution)/shard_map/jvp()/triangular_solve/custom-call.0 | solution.py:20
  407.9 1.5 fusion.66
  410.2 46.0 %gather_fusion.1 = s32[8192]{0:T(1024)S(1)} fusion(s32[8192]{0:T(1024)S(1)} %get-tuple-element.19, s32[8192]{0:T(1024)S(1)} %broadcast_clamp_fusion.3), kind=kCustom, calls=%fused_computation.1 | custom fusion | bytes 98304 | tf_op jit(solution)/shard_map/gather | solution.py:57
  456.3 45.5 %gather_fusion.8 = s32[8192]{0:T(1024)S(1)} fusion(s32[8192]{0:T(1024)S(1)} %get-tuple-element.4, s32[8192]{0:T(1024)S(1)} %broadcast_clamp_fusion.4), kind=kCustom, calls=%fused_computation.8 | custom fusion | bytes 98304 | tf_op jit(solution)/shard_map/gather | solution.py:81
  502.7 8.8 reshape.296
  511.4 11.0 copy.87
  522.4 38.4 %gather_fusion = bf16[8192,448]{1,0:T(8,128)(2,1)} fusion(bf16[8192,448]{1,0:T(8,128)(2,1)} %bitcast.194, s32[8192]{0:T(1024)S(1)} %broadcast_clamp_fusion.4), kind=kCustom, calls=%fused_computation | custom fusion | bytes 14712832 | tf_op jit(solution)/shard_map/gather | solution.py:47
  560.8 11.0 copy.89
  571.8 38.4 %gather_fusion.4 = bf16[8192,448]{1,0:T(8,128)(2,1)} fusion(bf16[8192,448]{1,0:T(8,128)(2,1)} %bitcast.193, s32[8192]{0:T(1024)S(1)} %broadcast_clamp_fusion.4), kind=kCustom, calls=%fused_computation.4 | custom fusion | bytes 14712832 | tf_op jit(solution)/shard_map/gather | solution.py:47
  610.2 9.6 convolution_convert_fusion.7
  619.8 38.4 %gather_fusion.2 = bf16[8192,448]{1,0:T(8,128)(2,1)} fusion(bf16[8192,448]{1,0:T(8,128)(2,1)} %bitcast.191, s32[8192]{0:T(1024)S(1)} %broadcast_clamp_fusion.2), kind=kCustom, calls=%fused_computation.2 | custom fusion | bytes 14712832 | tf_op jit(solution)/shard_map/gather | solution.py:47
  658.2 9.6 convolution_convert_fusion.5
  667.7 38.6 %gather_fusion.5 = bf16[8192,448]{1,0:T(8,128)(2,1)} fusion(bf16[8192,448]{1,0:T(8,128)(2,1)} %bitcast.188, s32[8192]{0:T(1024)S(1)} %broadcast_clamp_fusion.2), kind=kCustom, calls=%fused_computation.5 | custom fusion | bytes 14712832 | tf_op jit(solution)/shard_map/gather | solution.py:47
  706.3 9.6 convolution_convert_fusion.6
  715.9 38.4 %gather_fusion.3 = bf16[8192,448]{1,0:T(8,128)(2,1)} fusion(bf16[8192,448]{1,0:T(8,128)(2,1)} %bitcast.192, s32[8192]{0:T(1024)S(1)} %broadcast_clamp_fusion.1), kind=kCustom, calls=%fused_computation.3 | custom fusion | bytes 14712832 | tf_op jit(solution)/shard_map/gather | solution.py:60
  754.3 9.6 convolution_convert_fusion.4
  763.8 38.4 %gather_fusion.6 = bf16[8192,448]{1,0:T(8,128)(2,1)} fusion(bf16[8192,448]{1,0:T(8,128)(2,1)} %bitcast.189, s32[8192]{0:T(1024)S(1)} %broadcast_clamp_fusion.1), kind=kCustom, calls=%fused_computation.6 | custom fusion | bytes 14712832 | tf_op jit(solution)/shard_map/gather | solution.py:60
  802.2 9.3 convolution_bitcast_fusion.5
  811.5 8.2 multiply_convert_fusion
  819.8 6.0 fusion.1
  825.8 11.0 copy.94
  836.9 38.7 %gather_fusion.10 = bf16[8192,448]{1,0:T(8,128)(2,1)} fusion(bf16[8192,448]{1,0:T(8,128)(2,1)} %copy.94, s32[8192]{0:T(1024)S(1)} %copy-done.15), kind=kCustom, calls=%fused_computation.10 | custom fusion | bytes 14712832 | tf_op jit(solution)/shard_map/gather | solution.py:71
  875.6 10.1 convolution_bitcast_fusion
  885.8 9.7 convolution_convert_fusion.2
  895.4 38.4 %gather_fusion.11 = bf16[8192,448]{1,0:T(8,128)(2,1)} fusion(bf16[8192,448]{1,0:T(8,128)(2,1)} %bitcast.190, s32[8192]{0:T(1024)S(1)} %copy-done.16), kind=kCustom, calls=%fused_computation.11 | custom fusion | bytes 14712832 | tf_op jit(solution)/shard_map/gather | solution.py:71
  933.8 10.1 convolution_bitcast_fusion.1
  943.9 8.8 fusion
  952.7 11.0 copy.92
  963.7 38.5 %gather_fusion.7 = bf16[8192,448]{1,0:T(8,128)(2,1)} fusion(bf16[8192,448]{1,0:T(8,128)(2,1)} %copy.92, s32[8192]{0:T(1024)S(1)} %copy-done.15), kind=kCustom, calls=%fused_computation.7 | custom fusion | bytes 14712832 | tf_op jit(solution)/shard_map/gather | solution.py:71
  1002.3 10.2 convolution_bitcast_fusion.2
  1012.4 9.7 convolution_convert_fusion.3
  1022.1 38.4 %gather_fusion.9 = bf16[8192,448]{1,0:T(8,128)(2,1)} fusion(bf16[8192,448]{1,0:T(8,128)(2,1)} %bitcast.187, s32[8192]{0:T(1024)S(1)} %copy-done.16), kind=kCustom, calls=%fused_computation.9 | custom fusion | bytes 14712832 | tf_op jit(solution)/shard_map/gather | solution.py:71
  1060.5 10.1 convolution_bitcast_fusion.3
  1070.6 4.6 maximum_bitcast_fusion.1
  1075.2 3.6 maximum_bitcast_fusion
  1078.8 6.2 pad_maximum_fusion
  1085.1 79.7 %custom-call.26 = f32[2,2,4,1,64,64]{4,5,3,2,1,0:T(8,128)S(1)} custom-call(f32[2,2,4,1,64,64]{5,4,3,2,1,0:T(8,128)} %get-tuple-element.8), custom_call_target="InvertDiagBlocksLowerTriangular" | custom-call | tf_op jit(solution)/shard_map/transpose(jvp(jit(cholesky)))/triangular_solve/custom-call.0 | solution.py:18
  1164.9 199.9 %all-reduce.3.cloned.1.call-done = f32[2,2,128,64,64]{4,3,2,1,0:T(8,128)} async-done(((f32[2,2,128,64,64]{4,3,2,1,0:T(8,128)}), f32[2,2,128,64,64]{4,3,2,1,0:T(8,128)}) %all-reduce.3.cloned.1.call-update) | async-done | bytes 8388624
  1364.8 2.0 fusion.26
  1368.5 2.0 fusion.37
  1375.2 1.1 fusion.64
  1376.3 1.1 convolution_add_fusion.1
  (104 shorter events, 17.3 us)
Async XLA Ops:
  17.4 208.6 %all-to-all-start = ((bf16[256,32,448]{0,2,1:T(8,128)(2,1)}), bf16[256,32,448]{0,2,1:T(8,128)(2,1)}, u32[]{:S(2)}, u32[]{:S(2)}) async-start(bf16[256,32,448]{0,2,1:T(8,128)(2,1)} %bitcast.210), calls=%async_computation | async-start | bytes 14680064 | tf_op jit(solution)/shard_map/all_to_all | solution.py:110
  24.8 477.9 %all-gather.6.cloned.1.call-start = ((), (), s32[]{:S(2)}) async-start(), calls=%async_computation.3 | async-start | bytes 8650752 | tf_op jit(solution)/shard_map/all_gather | solution.py:108
  35.7 194.0 %copy-start.8 = (f32[2,2,4,64,64]{4,3,2,1,0:T(8,128)S(1)}, f32[2,2,4,64,64]{4,3,2,1,0:T(8,128)}, u32[]{:S(2)}) copy-start(f32[2,2,4,64,64]{4,3,2,1,0:T(8,128)} %param.13) | copy-start | bytes 786436
  226.0 334.8 %all-to-all-start.1 = ((bf16[256,32,448]{0,2,1:T(8,128)(2,1)}), bf16[256,32,448]{0,2,1:T(8,128)(2,1)}, u32[]{:S(2)}, u32[]{:S(2)}) async-start(bf16[256,32,448]{0,2,1:T(8,128)(2,1)} %bitcast.209), calls=%async_computation.1 | async-start | bytes 14680064 | tf_op jit(solution)/shard_map/all_to_all | solution.py:111
  229.7 179.8 %copy-start.23 = (s32[2,13]{1,0:T(2,128)S(1)}, s32[2,13]{1,0:T(2,128)}, u32[]{:S(2)}) copy-start(s32[2,13]{1,0:T(2,128)} %param.14) | copy-start | bytes 316
  229.7 380.5 %all-gather.4.cloned.1.call-start = ((), (), s32[]{:S(2)}) async-start(), calls=%async_computation.2 | async-start | bytes 8650752 | tf_op jit(solution)/shard_map/all_gather | solution.py:101
  230.0 179.5 %copy-start = (f32[2,2,4,64,64]{4,3,2,1,0:T(8,128)}, f32[2,2,4,64,64]{4,3,2,1,0:T(8,128)S(1)}, u32[]{:S(2)}) copy-start(f32[2,2,4,64,64]{4,3,2,1,0:T(8,128)S(1)} %bitcast_subtract_fusion.1) | copy-start | bytes 786436
  230.9 225.4 %copy-start.12 = (f32[64,64]{1,0:T(8,128)}, f32[64,64]{1,0:T(8,128)S(1)}, u32[]{:S(2)}) copy-start(f32[64,64]{1,0:T(8,128)S(1)} %get-tuple-element.21) | copy-start | bytes 49156
  324.8 1.9 copy-start.10
  325.1 1.6 copy-start.21
  325.7 1.0 copy-start.17
  405.3 50.9 %copy-start.2 = (f32[2,2,4,1,64,64]{4,5,3,2,1,0:T(8,128)}, f32[2,2,4,1,64,64]{4,5,3,2,1,0:T(8,128)S(1)}, u32[]{:S(2)}) copy-start(f32[2,2,4,1,64,64]{4,5,3,2,1,0:T(8,128)S(1)} %custom-call.22) | copy-start | bytes 786436
  407.0 0.9 copy-start.6
  409.4 955.3 %all-reduce.3.cloned.1.call-start = ((), (), s32[]{:S(2)}) async-start(), calls=%async_computation.4 | async-start | bytes 33554432
  410.2 46.0 %copy-start.14 = (s32[8192]{0:T(1024)}, s32[8192]{0:T(1024)S(1)}, u32[]{:S(2)}) copy-start(s32[8192]{0:T(1024)S(1)} %broadcast_clamp_fusion.3) | copy-start | bytes 98308
  802.2 9.3 copy-start.5
  802.2 17.5 %slice-start = ((s8[6291456]{0:T(1024)(128)(4,1)}), s8[4194304]{0:T(1024)(128)(4,1)S(1)}, s32[]{:S(2)}) async-start(s8[6291456]{0:T(1024)(128)(4,1)} %bitcast.211), calls=%async_computation.5 | async-start | bytes 8388608
  811.5 8.2 slice-start.1
  811.5 8.2 copy-start.24
  825.8 11.1 copy-start.15
  885.8 9.7 copy-start.16
  1070.6 4.6 copy-start.4
  1085.0 279.8 %copy-start.3 = (f32[2,2,4,1,64,64]{4,5,3,2,1,0:T(8,128)S(1)}, f32[2,2,4,1,64,64]{4,5,3,2,1,0:T(8,128)}, u32[]{:S(2)}) copy-start(f32[2,2,4,1,64,64]{4,5,3,2,1,0:T(8,128)} %copy-done.2) | copy-start | bytes 786436
  1085.0 281.8 %copy-start.7 = (f32[2,2,4,64,64]{4,3,2,1,0:T(8,128)S(1)}, f32[2,2,4,64,64]{4,3,2,1,0:T(8,128)}, u32[]{:S(2)}) copy-start(f32[2,2,4,64,64]{4,3,2,1,0:T(8,128)} %copy-done.6) | copy-start | bytes 786436
  1085.0 283.4 %copy-start.9 = (f32[2,2,4,64,64]{4,3,2,1,0:T(8,128)S(1)}, f32[2,2,4,64,64]{4,3,2,1,0:T(8,128)}, u32[]{:S(2)}) copy-start(f32[2,2,4,64,64]{4,3,2,1,0:T(8,128)} %get-tuple-element.15) | copy-start | bytes 786436
  1085.0 285.5 %copy-start.18 = (pred[64,64]{1,0:T(8,128)(4,1)S(1)}, pred[64,64]{1,0:T(8,128)(4,1)}, u32[]{:S(2)}) copy-start(pred[64,64]{1,0:T(8,128)(4,1)} %copy-done.17) | copy-start | bytes 12292
  1085.1 287.2 %copy-start.11 = (f32[2,2,4,64,64]{4,3,2,1,0:T(8,128)S(1)}, f32[2,2,4,64,64]{4,3,2,1,0:T(8,128)}, u32[]{:S(2)}) copy-start(f32[2,2,4,64,64]{4,3,2,1,0:T(8,128)} %copy-done.10) | copy-start | bytes 786436
  1085.1 287.2 %copy-start.22 = (pred[2,2,4]{2,1,0:T(4,128)(4,1)S(1)}, pred[2,2,4]{2,1,0:T(4,128)(4,1)}, u32[]{:S(2)}) copy-start(pred[2,2,4]{2,1,0:T(4,128)(4,1)} %copy-done.21) | copy-start | bytes 52
  1164.9 210.3 %copy-start.1 = (f32[2,2,4,64,64]{4,3,2,1,0:T(8,128)S(1)}, f32[2,2,4,64,64]{4,3,2,1,0:T(8,128)}, u32[]{:S(2)}) copy-start(f32[2,2,4,64,64]{4,3,2,1,0:T(8,128)} %copy-done) | copy-start | bytes 786436
  1164.9 210.3 %copy-start.19 = (pred[64,64]{1,0:T(8,128)(4,1)S(1)}, pred[64,64]{1,0:T(8,128)(4,1)}, u32[]{:S(2)}) copy-start(pred[64,64]{1,0:T(8,128)(4,1)} %get-tuple-element.12) | copy-start | bytes 12292
  1164.9 210.3 %copy-start.20 = (pred[64,64]{1,0:T(8,128)(4,1)S(1)}, pred[64,64]{1,0:T(8,128)(4,1)}, u32[]{:S(2)}) copy-start(pred[64,64]{1,0:T(8,128)(4,1)} %get-tuple-element.13) | copy-start | bytes 12292
  1368.5 8.9 copy-start.13
Sparse Core Ops, SparseCore 0:
  28.5 163.7 all-gather.5
  409.6 78.5 all-gather.3
  1085.2 279.5 all-reduce.2
where the time goes:
time: 1400 us; the launch traced here: 1390 us
  local copies, waits for them, and re-layouts  551 us (39%)
  waiting for transfers between devices  391 us (28%)
  other arithmetic  271 us (19%)
  matrix products  149 us (11%)
  between operations  14.6 us (1%)
    unnamed x4, waiting for transfers between devices  201 us
    all_to_all x1, waiting for transfers between devices, shards(): lax.all_to_all(gate_weight, 'rows', split_axis=1, concat_axis=0, tiled=True)  190 us
    another operation x6, other arithmetic, cayley(): lower_factor = jnp.linalg.cholesky(normal)  175 us
    gather x4, local copies, waits for them, and re-layouts, unrotate(): permuted = current[index]  154 us
    gather x4, local copies, waits for them, and re-layouts, rotate_columns(): permuted = current[index]  154 us
    another operation x1, other arithmetic, cayley(): lax.linalg.triangular_solve(lower_factor, halfway, left_side=True, lower=...  78.6 us
    gather x2, local copies, waits for them, and re-layouts, rotate_columns(): return (current[index], kept_inputs)  76.7 us
    gather x1, local copies, waits for them, and re-layouts, rotate_columns(): index = inverses[section_at][orders[section_at + 1]]  46 us
  transfers between devices with their start and end apart: 5, of which 2 were waited for; matrix products, arithmetic and copies ran while one was open for 34% of the time, Pallas kernels for 0%

commit v1 on v0

--- a/solution.py
+++ b/solution.py
@@ -2,6 +2,7 @@
 import jax.numpy as jnp
 from jax import lax
 from jax.sharding import PartitionSpec as P
+from jax.lax import all_to_all, axis_size
 
 
 def cayley(skew_blocks):
@@ -107,7 +108,10 @@
     ]
     all_tokens = lax.all_gather(tokens, "rows", axis=0, tiled=True)
     gate_cols, up_cols = (
-        lax.all_to_all(gate_weight, "rows", split_axis=1, concat_axis=0, tiled=True),
+        jnp.concatenate(
+            all_to_all(jnp.stack(jnp.split(gate_weight, axis_size("rows"), axis=1)), "rows", 0, 0),
+            axis=0,
+        ),
         lax.all_to_all(up_weight, "rows", split_axis=1, concat_axis=0, tiled=True),
     )
     rotated_gate, gate_inputs = rotate_columns(gate_cols, rotation[0], orders, inverses)

time: 1400 us -> 1470 us (1.050)
  local copies, waits for them, and re-layouts: 551 us -> 626 us
    unnamed x58 -> x122, local copies, waits for them, and re-layouts: 30.3 us -> 96.1 us
  transfers between devices with their start and end apart: 5 -> 5, of which waited for: 2 -> 2; matrix products, arithmetic and copies ran while one was open for 34% -> 32% of each run, Pallas kernels for 0% -> 0%
where the time goes in v1:
time: 1470 us; the launch traced here: 1460 us
  local copies, waits for them, and re-layouts  626 us (43%)
  waiting for transfers between devices  391 us (27%)
  other arithmetic  271 us (18%)
  matrix products  149 us (10%)
  between operations  15 us (1%)
    unnamed x4, waiting for transfers between devices  200 us
    all_to_all x1, waiting for transfers between devices, shards(): all_to_all(jnp.stack(jnp.split(gate_weight, axis_size('rows'), axis=1)),...  190 us
    another operation x6, other arithmetic, cayley(): lower_factor = jnp.linalg.cholesky(normal)  175 us
    gather x4, local copies, waits for them, and re-layouts, unrotate(): permuted = current[index]  153 us
    gather x4, local copies, waits for them, and re-layouts, rotate_columns(): permuted = current[index]  153 us
    unnamed x122, local copies, waits for them, and re-layouts  96.1 us
    another operation x1, other arithmetic, cayley(): lax.linalg.triangular_solve(lower_factor, halfway, left_side=True, lower=...  78.6 us
    gather x2, local copies, waits for them, and re-layouts, rotate_columns(): return (current[index], kept_inputs)  76.4 us
  transfers between devices with their start and end apart: 5, of which 2 were waited for; matrix products, arithmetic and copies ran while one was open for 32% of the time, Pallas kernels for 0%

profile of v1, /device:TPU:0, one launch (start us, length us, event | category | flops | bytes accessed | tf_op | source)
XLA Modules:
  0.0 1462.4 jit_solution(16187743604003416157)
XLA Ops:
  7.2 4.6 fusion.67
  11.8 5.3 fusion.66
  43.6 1.8 copy.193
  45.4 1.8 copy.194
  93.9 7.4 all-to-all-start
  102.0 10.2 copy.147
  112.2 190.3 %all-to-all-done = bf16[32,256,448]{1,2,0:T(8,128)(2,1)} async-done(((bf16[32,256,448]{1,2,0:T(8,128)(2,1)}), bf16[32,256,448]{1,2,0:T(8,128)(2,1)}, u32[]{:S(2)}, u32[]{:S(2)}) %all-to-all-start) | async-done | bytes 7340064 | tf_op jit(solution)/shard_map/all_to_all | solution.py:112
  302.5 3.7 all-to-all-start.1
  308.0 93.8 %custom-call.14 = f32[2,2,4,64,64]{4,3,2,1,0:T(8,128)S(1)} custom-call(f32[2,2,4,64,64]{4,3,2,1,0:T(8,128)S(1)} %fusion.35), custom_call_target="Cholesky" | custom-call | tf_op jit(solution)/shard_map/jvp(jit(cholesky))/cholesky | solution.py:19
  403.7 78.6 %custom-call.22 = f32[2,2,4,1,64,64]{4,5,3,2,1,0:T(8,128)S(1)} custom-call(f32[2,2,4,1,64,64]{5,4,3,2,1,0:T(8,128)S(1)} %get-tuple-element.41), custom_call_target="InvertDiagBlocksLowerTriangular" | custom-call | tf_op jit(solution)/shard_map/jvp()/triangular_solve/custom-call.0 | solution.py:21
  487.2 45.7 %gather_fusion.1 = s32[8192]{0:T(1024)S(1)} fusion(s32[8192]{0:T(1024)S(1)} %get-tuple-element.51, s32[8192]{0:T(1024)S(1)} %broadcast_clamp_fusion.3), kind=kCustom, calls=%fused_computation.1 | custom fusion | bytes 98304 | tf_op jit(solution)/shard_map/gather | solution.py:58
  533.0 45.5 %gather_fusion.8 = s32[8192]{0:T(1024)S(1)} fusion(s32[8192]{0:T(1024)S(1)} %get-tuple-element.4, s32[8192]{0:T(1024)S(1)} %broadcast_clamp_fusion.4), kind=kCustom, calls=%fused_computation.8 | custom fusion | bytes 98304 | tf_op jit(solution)/shard_map/gather | solution.py:82
  579.3 8.7 reshape.297
  588.1 11.0 copy.146
  599.0 38.3 %gather_fusion = bf16[8192,448]{1,0:T(8,128)(2,1)} fusion(bf16[8192,448]{1,0:T(8,128)(2,1)} %bitcast.256, s32[8192]{0:T(1024)S(1)} %broadcast_clamp_fusion.4), kind=kCustom, calls=%fused_computation | custom fusion | bytes 14712832 | tf_op jit(solution)/shard_map/gather | solution.py:48
  637.3 11.0 copy.148
  648.3 38.2 %gather_fusion.4 = bf16[8192,448]{1,0:T(8,128)(2,1)} fusion(bf16[8192,448]{1,0:T(8,128)(2,1)} %bitcast.255, s32[8192]{0:T(1024)S(1)} %broadcast_clamp_fusion.4), kind=kCustom, calls=%fused_computation.4 | custom fusion | bytes 14712832 | tf_op jit(solution)/shard_map/gather | solution.py:48
  686.5 9.6 convolution_convert_fusion.7
  696.1 38.2 %gather_fusion.2 = bf16[8192,448]{1,0:T(8,128)(2,1)} fusion(bf16[8192,448]{1,0:T(8,128)(2,1)} %bitcast.253, s32[8192]{0:T(1024)S(1)} %broadcast_clamp_fusion.2), kind=kCustom, calls=%fused_computation.2 | custom fusion | bytes 14712832 | tf_op jit(solution)/shard_map/gather | solution.py:48
  734.4 9.6 convolution_convert_fusion.5
  743.9 38.4 %gather_fusion.5 = bf16[8192,448]{1,0:T(8,128)(2,1)} fusion(bf16[8192,448]{1,0:T(8,128)(2,1)} %bitcast.250, s32[8192]{0:T(1024)S(1)} %broadcast_clamp_fusion.2), kind=kCustom, calls=%fused_computation.5 | custom fusion | bytes 14712832 | tf_op jit(solution)/shard_map/gather | solution.py:48
  782.4 9.6 convolution_convert_fusion.6
  792.0 38.2 %gather_fusion.3 = bf16[8192,448]{1,0:T(8,128)(2,1)} fusion(bf16[8192,448]{1,0:T(8,128)(2,1)} %bitcast.254, s32[8192]{0:T(1024)S(1)} %broadcast_clamp_fusion.1), kind=kCustom, calls=%fused_computation.3 | custom fusion | bytes 14712832 | tf_op jit(solution)/shard_map/gather | solution.py:61
  830.2 9.6 convolution_convert_fusion.4
  839.8 38.2 %gather_fusion.6 = bf16[8192,448]{1,0:T(8,128)(2,1)} fusion(bf16[8192,448]{1,0:T(8,128)(2,1)} %bitcast.251, s32[8192]{0:T(1024)S(1)} %broadcast_clamp_fusion.1), kind=kCustom, calls=%fused_computation.6 | custom fusion | bytes 14712832 | tf_op jit(solution)/shard_map/gather | solution.py:61
  878.0 9.5 convolution_bitcast_fusion.5
  887.4 8.2 multiply_convert_fusion
  895.7 6.0 fusion.1
  901.7 11.1 copy.153
  912.8 38.4 %gather_fusion.10 = bf16[8192,448]{1,0:T(8,128)(2,1)} fusion(bf16[8192,448]{1,0:T(8,128)(2,1)} %copy.153, s32[8192]{0:T(1024)S(1)} %copy-done.16), kind=kCustom, calls=%fused_computation.10 | custom fusion | bytes 14712832 | tf_op jit(solution)/shard_map/gather | solution.py:72
  951.2 10.2 convolution_bitcast_fusion
  961.4 9.7 convolution_convert_fusion.2
  971.0 38.2 %gather_fusion.11 = bf16[8192,448]{1,0:T(8,128)(2,1)} fusion(bf16[8192,448]{1,0:T(8,128)(2,1)} %bitcast.252, s32[8192]{0:T(1024)S(1)} %copy-done.17), kind=kCustom, calls=%fused_computation.11 | custom fusion | bytes 14712832 | tf_op jit(solution)/shard_map/gather | solution.py:72
  1009.3 10.1 convolution_bitcast_fusion.1
  1019.4 8.8 fusion
  1028.2 11.1 copy.151
  1039.3 38.4 %gather_fusion.7 = bf16[8192,448]{1,0:T(8,128)(2,1)} fusion(bf16[8192,448]{1,0:T(8,128)(2,1)} %copy.151, s32[8192]{0:T(1024)S(1)} %copy-done.16), kind=kCustom, calls=%fused_computation.7 | custom fusion | bytes 14712832 | tf_op jit(solution)/shard_map/gather | solution.py:72
  1077.7 10.2 convolution_bitcast_fusion.2
  1087.9 9.7 convolution_convert_fusion.3
  1097.5 38.2 %gather_fusion.9 = bf16[8192,448]{1,0:T(8,128)(2,1)} fusion(bf16[8192,448]{1,0:T(8,128)(2,1)} %bitcast.249, s32[8192]{0:T(1024)S(1)} %copy-done.17), kind=kCustom, calls=%fused_computation.9 | custom fusion | bytes 14712832 | tf_op jit(solution)/shard_map/gather | solution.py:72
  1135.8 10.1 convolution_bitcast_fusion.3
  1145.9 4.6 maximum_bitcast_fusion.1
  1150.5 3.6 maximum_bitcast_fusion
  1154.1 6.2 pad_maximum_fusion
  1160.4 79.7 %custom-call.26 = f32[2,2,4,1,64,64]{4,5,3,2,1,0:T(8,128)S(1)} custom-call(f32[2,2,4,1,64,64]{5,4,3,2,1,0:T(8,128)} %get-tuple-element.40), custom_call_target="InvertDiagBlocksLowerTriangular" | custom-call | tf_op jit(solution)/shard_map/transpose(jvp(jit(cholesky)))/triangular_solve/custom-call.0 | solution.py:19
  1240.2 199.5 %all-reduce.3.cloned.1.call-done = f32[2,2,128,64,64]{4,3,2,1,0:T(8,128)} async-done(((f32[2,2,128,64,64]{4,3,2,1,0:T(8,128)}), f32[2,2,128,64,64]{4,3,2,1,0:T(8,128)}) %all-reduce.3.cloned.1.call-update) | async-done | bytes 8388624
  1439.7 2.0 fusion.26
  1443.5 2.0 fusion.37
  (171 shorter events, 94.6 us)
Async XLA Ops:
  55.0 29.6 %copy-start.12 = (bf16[256,448]{0,1:T(8,128)(2,1)S(1)}, bf16[256,448]{0,1:T(8,128)(2,1)}, u32[]{:S(2)}) copy-start(bf16[256,448]{0,1:T(8,128)(2,1)} %copy.198) | copy-start | bytes 688132
  93.9 208.6 %all-to-all-start = ((bf16[32,256,448]{1,2,0:T(8,128)(2,1)}), bf16[32,256,448]{1,2,0:T(8,128)(2,1)}, u32[]{:S(2)}, u32[]{:S(2)}) async-start(bf16[32,256,448]{1,2,0:T(8,128)(2,1)} %bitcast_dynamic-update-slice_fusion), calls=%async_computation | async-start | bytes 14680064 | tf_op jit(solution)/shard_map/all_to_all | solution.py:112
  101.3 478.0 %all-gather.6.cloned.1.call-start = ((), (), s32[]{:S(2)}) async-start(), calls=%async_computation.3 | async-start | bytes 8650752 | tf_op jit(solution)/shard_map/all_gather | solution.py:109
  112.2 194.5 %copy-start.8 = (f32[2,2,4,64,64]{4,3,2,1,0:T(8,128)S(1)}, f32[2,2,4,64,64]{4,3,2,1,0:T(8,128)}, u32[]{:S(2)}) copy-start(f32[2,2,4,64,64]{4,3,2,1,0:T(8,128)} %param.13) | copy-start | bytes 786436
  302.5 334.8 %all-to-all-start.1 = ((bf16[256,32,448]{0,2,1:T(8,128)(2,1)}), bf16[256,32,448]{0,2,1:T(8,128)(2,1)}, u32[]{:S(2)}, u32[]{:S(2)}) async-start(bf16[256,32,448]{0,2,1:T(8,128)(2,1)} %bitcast.271), calls=%async_computation.1 | async-start | bytes 14680064 | tf_op jit(solution)/shard_map/all_to_all | solution.py:115
  306.2 180.3 %copy-start.24 = (s32[2,13]{1,0:T(2,128)S(1)}, s32[2,13]{1,0:T(2,128)}, u32[]{:S(2)}) copy-start(s32[2,13]{1,0:T(2,128)} %param.14) | copy-start | bytes 316
  306.2 380.3 %all-gather.4.cloned.1.call-start = ((), (), s32[]{:S(2)}) async-start(), calls=%async_computation.2 | async-start | bytes 8650752 | tf_op jit(solution)/shard_map/all_gather | solution.py:102
  307.0 179.5 %copy-start = (f32[2,2,4,64,64]{4,3,2,1,0:T(8,128)}, f32[2,2,4,64,64]{4,3,2,1,0:T(8,128)S(1)}, u32[]{:S(2)}) copy-start(f32[2,2,4,64,64]{4,3,2,1,0:T(8,128)S(1)} %bitcast_subtract_fusion.1) | copy-start | bytes 786436
  307.9 225.0 %copy-start.13 = (f32[64,64]{1,0:T(8,128)}, f32[64,64]{1,0:T(8,128)S(1)}, u32[]{:S(2)}) copy-start(f32[64,64]{1,0:T(8,128)S(1)} %get-tuple-element.53) | copy-start | bytes 49156
  401.8 1.9 copy-start.10
  402.0 1.6 copy-start.22
  402.7 1.0 copy-start.18
  482.3 50.6 %copy-start.2 = (f32[2,2,4,1,64,64]{4,5,3,2,1,0:T(8,128)}, f32[2,2,4,1,64,64]{4,5,3,2,1,0:T(8,128)S(1)}, u32[]{:S(2)}) copy-start(f32[2,2,4,1,64,64]{4,5,3,2,1,0:T(8,128)S(1)} %custom-call.22) | copy-start | bytes 786436
  484.0 0.8 copy-start.6
  486.4 953.3 %all-reduce.3.cloned.1.call-start = ((), (), s32[]{:S(2)}) async-start(), calls=%async_computation.4 | async-start | bytes 33554432
  487.2 45.7 %copy-start.15 = (s32[8192]{0:T(1024)}, s32[8192]{0:T(1024)S(1)}, u32[]{:S(2)}) copy-start(s32[8192]{0:T(1024)S(1)} %broadcast_clamp_fusion.3) | copy-start | bytes 98308
  878.0 9.5 copy-start.5
  878.0 17.7 %slice-start = ((s8[6291456]{0:T(1024)(128)(4,1)}), s8[4194304]{0:T(1024)(128)(4,1)S(1)}, s32[]{:S(2)}) async-start(s8[6291456]{0:T(1024)(128)(4,1)} %bitcast.272), calls=%async_computation.5 | async-start | bytes 8388608
  887.4 8.2 slice-start.1
  887.4 8.2 copy-start.25
  901.7 11.1 copy-start.16
  961.4 9.7 copy-start.17
  1145.9 4.6 copy-start.4
  1160.3 279.4 %copy-start.3 = (f32[2,2,4,1,64,64]{4,5,3,2,1,0:T(8,128)S(1)}, f32[2,2,4,1,64,64]{4,5,3,2,1,0:T(8,128)}, u32[]{:S(2)}) copy-start(f32[2,2,4,1,64,64]{4,5,3,2,1,0:T(8,128)} %copy-done.2) | copy-start | bytes 786436
  1160.3 281.5 %copy-start.7 = (f32[2,2,4,64,64]{4,3,2,1,0:T(8,128)S(1)}, f32[2,2,4,64,64]{4,3,2,1,0:T(8,128)}, u32[]{:S(2)}) copy-start(f32[2,2,4,64,64]{4,3,2,1,0:T(8,128)} %copy-done.6) | copy-start | bytes 786436
  1160.3 283.1 %copy-start.9 = (f32[2,2,4,64,64]{4,3,2,1,0:T(8,128)S(1)}, f32[2,2,4,64,64]{4,3,2,1,0:T(8,128)}, u32[]{:S(2)}) copy-start(f32[2,2,4,64,64]{4,3,2,1,0:T(8,128)} %get-tuple-element.47) | copy-start | bytes 786436
  1160.3 285.2 %copy-start.19 = (pred[64,64]{1,0:T(8,128)(4,1)S(1)}, pred[64,64]{1,0:T(8,128)(4,1)}, u32[]{:S(2)}) copy-start(pred[64,64]{1,0:T(8,128)(4,1)} %copy-done.18) | copy-start | bytes 12292
  1160.3 286.8 %copy-start.11 = (f32[2,2,4,64,64]{4,3,2,1,0:T(8,128)S(1)}, f32[2,2,4,64,64]{4,3,2,1,0:T(8,128)}, u32[]{:S(2)}) copy-start(f32[2,2,4,64,64]{4,3,2,1,0:T(8,128)} %copy-done.10) | copy-start | bytes 786436
  1160.4 286.8 %copy-start.23 = (pred[2,2,4]{2,1,0:T(4,128)(4,1)S(1)}, pred[2,2,4]{2,1,0:T(4,128)(4,1)}, u32[]{:S(2)}) copy-start(pred[2,2,4]{2,1,0:T(4,128)(4,1)} %copy-done.22) | copy-start | bytes 52
  1240.2 210.0 %copy-start.1 = (f32[2,2,4,64,64]{4,3,2,1,0:T(8,128)S(1)}, f32[2,2,4,64,64]{4,3,2,1,0:T(8,128)}, u32[]{:S(2)}) copy-start(f32[2,2,4,64,64]{4,3,2,1,0:T(8,128)} %copy-done) | copy-start | bytes 786436
  1240.2 210.0 %copy-start.20 = (pred[64,64]{1,0:T(8,128)(4,1)S(1)}, pred[64,64]{1,0:T(8,128)(4,1)}, u32[]{:S(2)}) copy-start(pred[64,64]{1,0:T(8,128)(4,1)} %get-tuple-element.44) | copy-start | bytes 12292
  1240.2 210.0 %copy-start.21 = (pred[64,64]{1,0:T(8,128)(4,1)S(1)}, pred[64,64]{1,0:T(8,128)(4,1)}, u32[]{:S(2)}) copy-start(pred[64,64]{1,0:T(8,128)(4,1)} %get-tuple-element.45) | copy-start | bytes 12292
  1443.5 8.9 copy-start.14
Sparse Core Ops, SparseCore 0:
  105.0 163.7 all-gather.5
  486.5 78.5 all-gather.3
  1160.5 279.2 all-reduce.2
